TPU v7x, 32 devices: a whole 2x2x4 slice. The times are simulated.
32 devices in a mesh: rows: 8 (over z, y), cols: 4 (over x, core).
Axes of the slice: x: 2, y: 2, z: 4, core: 2. Of those that a mesh axis runs over, the one named last changes fastest.
Arguments:
- right_leaf: float32 [4, 2048, 128], P(None, 'rows'), may hold values from -6 to 6
- right_mid: float32 [2, 4096, 128], P(None, 'rows'), may hold values from -6 to 6
- right_root: float32 [8192, 128], P('rows'), may hold values from -6 to 6
- inverse_leaf: float32 [4, 2048, 2048], P(None, 'rows', 'cols'), may hold values from -1 to 2, as said below
- inverse_mid: float32 [2, 4096, 4096], P(None, 'rows', 'cols'), may hold values from -1 to 2, as said below
- inverse_root: float32 [8192, 8192], P('rows', 'cols'), may hold values from -1 to 2, as said below
- leaf_to_mid: float32 [4, 4096, 2048], P(None, 'rows', 'cols'), may hold values from -0.125 to 0.125
- leaf_to_root: float32 [4, 8192, 2048], P(None, 'rows', 'cols'), may hold values from -0.125 to 0.125
- mid_to_root: float32 [2, 8192, 4096], P(None, 'rows', 'cols'), may hold values from -0.09375 to 0.09375
- mask_leaf_mid: int32 [4, 32, 16], replicated, may hold values 0 or 1
- mask_leaf_root: int32 [4, 64, 16], replicated, may hold values 0 or 1
- mask_mid_root: int32 [2, 64, 32], replicated, may hold values 0 or 1
Outputs:
- solved_leaf: float32 [4, 2048, 128], P(None, 'rows')
- solved_mid: float32 [2, 4096, 128], P(None, 'rows')
- solved_root: float32 [8192, 128], P('rows')
Inputs may be any that keep to these rules, and one draw needn't show every extreme that they name: `inverse_leaf`: lower triangular, with its diagonal between 0.5 and 2. `inverse_mid`: lower triangular, with its diagonal between 0.5 and 2. `inverse_root`: lower triangular, with its diagonal between 0.5 and 2.
All inputs are finite; a program needn't handle non-finite values.
Results may differ from a plain program's by a relative error of at most 0.00014.
Values sent between devices are 32-bit elements; how exact they have to be, the bound alone decides.
No kernel may reach another device: no remote copies, remote signals or barrier semaphores. Data moves between devices by JAX's collectives and lax.ppermute only.
A program may use at most 128 MiB of HBM per device.

v0:
```python
import jax
import jax.numpy as jnp
from jax import lax
from jax.sharding import PartitionSpec as P

TILE = 128


def product(matrix, vector):
    return jnp.einsum(
        "src,sck->srk",
        matrix,
        vector,
        precision=lax.Precision.HIGHEST,
        preferred_element_type=jnp.float32,
    )


def own_columns(gathered):
    col_width = gathered.shape[1] // lax.axis_size("cols")
    return lax.dynamic_slice_in_dim(gathered, lax.axis_index("cols") * col_width, col_width, 1)


def masked(values, pattern):
    rows_dev = values.shape[1]
    cols_dev = values.shape[2]
    row_ids = lax.axis_index("rows") * rows_dev + lax.iota(jnp.int32, rows_dev)
    col_ids = lax.axis_index("cols") * cols_dev + lax.iota(jnp.int32, cols_dev)
    row_hot = (row_ids[:, None] // TILE == lax.iota(jnp.int32, pattern.shape[1])[None, :]).astype(
        jnp.float32
    )
    col_hot = (col_ids[:, None] // TILE == lax.iota(jnp.int32, pattern.shape[2])[None, :]).astype(
        jnp.float32
    )
    expanded = jnp.einsum("ra,sab,cb->src", row_hot, pattern.astype(jnp.float32), col_hot)
    return values * expanded


def fetch_columns(block):
    gathered = lax.all_gather(block, "rows", axis=1, tiled=True)
    return own_columns(gathered)


def solve_block(residual, inverse, spread_needed):
    partial_value = product(inverse, fetch_columns(residual))
    solved = lax.psum(partial_value, "cols")
    spread = fetch_columns(solved) if spread_needed else solved
    return (solved, spread)


def body(
    right_leaf,
    right_mid,
    right_root,
    inverse_leaf,
    inverse_mid,
    inverse_root,
    leaf_to_mid,
    leaf_to_root,
    mid_to_root,
    mask_leaf_mid,
    mask_leaf_root,
    mask_mid_root,
):
    factor_lm = masked(leaf_to_mid, mask_leaf_mid)
    factor_lr = masked(leaf_to_root, mask_leaf_root)
    factor_mr = masked(mid_to_root, mask_mid_root)
    solved_leaf, leaf_columns = solve_block(right_leaf, inverse_leaf, True)
    mid_terms = product(factor_lm, leaf_columns)
    mid_part = mid_terms.reshape(2, 2, mid_terms.shape[1], mid_terms.shape[2]).sum(axis=1)
    root_part = product(factor_lr, leaf_columns).sum(axis=0)[None]
    mid_summed, root_summed = lax.psum((mid_part, root_part), "cols")
    resid_mid = right_mid - mid_summed
    solved_mid, mid_columns = solve_block(resid_mid, inverse_mid, True)
    root_more = product(factor_mr, mid_columns).sum(axis=0)[None]
    resid_root = right_root[None] - root_summed - lax.psum(root_more, "cols")
    solved_root, unused_spread = solve_block(resid_root, inverse_root[None], False)
    return (solved_leaf, solved_mid, solved_root[0])


def solution(mesh):
    placed = (
        P(None, "rows", None),
        P(None, "rows", None),
        P("rows", None),
        P(None, "rows", "cols"),
        P(None, "rows", "cols"),
        P("rows", "cols"),
        P(None, "rows", "cols"),
        P(None, "rows", "cols"),
        P(None, "rows", "cols"),
        P(),
        P(),
        P(),
    )
    return jax.shard_map(
        body,
        mesh=mesh,
        in_specs=placed,
        out_specs=(P(None, "rows", None), P(None, "rows", None), P("rows", None)),
        check_vma=False,
    )
```

profile of v0, /device:TPU:0, one launch (start us, length us, event | category | flops | bytes accessed | tf_op | source)
XLA Modules:
  0.0 608.7 jit_solution(15092546820964897420)
XLA Ops:
  7.2 0.0 copy-start
  7.2 0.0 copy-start.6
  7.2 0.0 all-gather.6.cloned.1.call-start
  7.2 2.2 copy.32
  9.4 0.0 all-gather.6.cloned.1.call-update
  9.4 0.0 all-reduce.7.cloned.1.call-start
  9.5 78.9 %all-gather.6.cloned.1.call-done = f32[4,2048,128]{1,2,0:T(8,128)} async-done(((f32[4,256,128]{1,2,0:T(8,128)}), f32[4,2048,128]{1,2,0:T(8,128)}) %all-gather.6.cloned.1.call-update) | async-done | bytes 4194320 | tf_op jit(solution)/shard_map/all_gather | solution.py:40
  88.4 0.0 copy-done
  88.4 4.2 convolution_bitcast_fusion.1
  92.6 0.0 all-reduce.7.cloned.1.call-update
  92.6 0.0 all-gather.8.cloned.1.call-start
  92.7 31.4 %all-reduce.7.cloned.1.call-done = f32[4,256,128]{1,2,0:T(8,128)} async-done(((f32[4,256,128]{1,2,0:T(8,128)}), f32[4,256,128]{1,2,0:T(8,128)}) %all-reduce.7.cloned.1.call-update) | async-done | bytes 524304 | tf_op jit(solution)/shard_map/psum | solution.py:46
  124.1 0.0 all-gather.8.cloned.1.call-update
  124.1 0.0 all-reduce.9.cloned.1.call-start
  124.2 0.0 copy-done.6
  124.3 0.2 fusion.32
  124.4 2.7 fusion.37
  127.1 74.1 %all-gather.8.cloned.1.call-done = f32[4,2048,128]{1,2,0:T(8,128)} async-done(((f32[4,256,128]{1,2,0:T(8,128)}), f32[4,2048,128]{1,2,0:T(8,128)}) %all-gather.8.cloned.1.call-update) | async-done | bytes 4194320 | tf_op jit(solution)/shard_map/all_gather | solution.py:40
  201.2 7.5 %bitcast_reduce_fusion = f32[2,512,128]{2,1,0:T(8,128)S(1)} fusion(f32[4,2048,128]{1,2,0:T(8,128)} %all-gather.8.cloned.1.call-done, s32[]{:T(128)S(6)} %select_n.49, f32[4,512,512]{2,1,0:T(8,128)} %param.18, f32[4,512,512]{2,1,0:T(8,128)} %fusion.37), kind=kOutput, calls=%fused_computation.12 | convolution fusion | flops 1611792384 | bytes 9961476 | tf_op jit(solution)/shard_map/src,sck->srk/dot_general | solution.py:10
  208.7 1.0 copy.34
  209.7 0.0 all-reduce.9.cloned.1.call-update
  209.7 0.0 all-gather.10.cloned.1.call-start
  209.8 0.0 copy-done.4
  209.8 0.2 copy.35
  210.0 0.0 copy-start.7
  210.0 0.0 copy-start.8
  210.0 31.2 %all-reduce.9.cloned.1.call-done = f32[2,512,128]{1,2,0:T(8,128)} async-done(((f32[2,512,128]{1,2,0:T(8,128)}), f32[2,512,128]{1,2,0:T(8,128)}) %all-reduce.9.cloned.1.call-update) | async-done | bytes 524304 | tf_op jit(solution)/shard_map/psum | solution.py:72
  241.3 1.9 sub.35
  243.2 0.0 all-gather.10.cloned.1.call-update
  243.2 0.0 all-reduce.11.cloned.1.call-start
  243.3 74.0 %all-gather.10.cloned.1.call-done = f32[2,4096,128]{1,2,0:T(8,128)} async-done(((f32[2,512,128]{1,2,0:T(8,128)}), f32[2,4096,128]{1,2,0:T(8,128)}) %all-gather.10.cloned.1.call-update) | async-done | bytes 4194320 | tf_op jit(solution)/shard_map/all_gather | solution.py:40
  317.3 7.7 %convolution_bitcast_fusion.2 = f32[2,512,128]{1,2,0:T(8,128)} fusion(f32[2,512,1024]{2,1,0:T(8,128)} %param.16, f32[2,4096,128]{1,2,0:T(8,128)} %all-gather.10.cloned.1.call-done, s32[]{:T(128)S(6)} %select_n.52), kind=kOutput, calls=%fused_computation.10 | convolution fusion | flops 1610612736 | bytes 5767172 | tf_op jit(solution)/shard_map/src,sck->srk/dot_general | solution.py:10
  325.0 0.0 all-reduce.11.cloned.1.call-update
  325.0 0.0 all-gather.12.cloned.1.call-start
  325.0 31.5 %all-reduce.11.cloned.1.call-done = f32[2,512,128]{1,2,0:T(8,128)} async-done(((f32[2,512,128]{1,2,0:T(8,128)}), f32[2,512,128]{1,2,0:T(8,128)}) %all-reduce.11.cloned.1.call-update) | async-done | bytes 524304 | tf_op jit(solution)/shard_map/psum | solution.py:46
  356.6 0.0 all-gather.12.cloned.1.call-update
  356.6 0.2 all-reduce.15.cloned.1.call-start
  356.8 0.0 copy-done.7
  356.9 0.0 copy-done.8
  356.9 0.2 fusion.24
  357.1 0.2 fusion.25
  357.3 0.0 slice-start
  357.3 1.3 fusion.35
  358.6 0.0 slice-start.1
  358.6 4.5 fusion.29
  363.1 0.0 slice-done
  363.1 8.7 %fusion.6 = f32[1,1024,128]{2,1,0:T(8,128)} fusion(f32[4,1024,512]{2,1,0:T(8,128)S(1)} %bitcast.56, f32[4,1024,512]{2,1,0:T(8,128)S(1)} %fusion.35, f32[4,2048,128]{1,2,0:T(8,128)} %all-gather.8.cloned.1.call-done, s32[]{:T(128)S(6)} %select_n.49), kind=kOutput, calls=%fused_computation.6 | convolution fusion | flops 3223322624 | bytes 18350084 | tf_op jit(solution)/shard_map/src,sck->srk/dot_general | solution.py:10
  371.9 60.3 %all-gather.12.cloned.1.call-done = f32[2,4096,128]{1,2,0:T(8,128)} async-done(((f32[2,512,128]{1,2,0:T(8,128)}), f32[2,4096,128]{1,2,0:T(8,128)}) %all-gather.12.cloned.1.call-update) | async-done | bytes 4194320 | tf_op jit(solution)/shard_map/all_gather | solution.py:40
  432.2 11.2 %fusion.9 = f32[1,1024,128]{2,1,0:T(8,128)} fusion(f32[2,1024,1024]{2,1,0:T(8,128)} %param.20, f32[2,1024,1024]{2,1,0:T(8,128)} %fusion.29, f32[2,4096,128]{1,2,0:T(8,128)} %all-gather.12.cloned.1.call-done, s32[]{:T(128)S(6)} %select_n.52), kind=kOutput, calls=%fused_computation.7 | convolution fusion | flops 3223322624 | bytes 18350084 | tf_op jit(solution)/shard_map/src,sck->srk/dot_general | solution.py:10
  443.4 0.0 all-reduce.15.cloned.1.call-update
  443.5 0.0 all-gather.14.cloned.1.call-start
  443.5 34.5 %all-reduce.15.cloned.1.call-done = (f32[1,1024,128]{2,1,0:T(8,128)}, f32[1,1024,128]{2,1,0:T(8,128)}) async-done(((f32[1,1024,128]{2,1,0:T(8,128)}, f32[1,1024,128]{2,1,0:T(8,128)}), (f32[1,1024,128]{2,1,0:T(8,128)}, f32[1,1024,128]{2,1,0:T(8,128)})) %all-reduce.15.cloned.1.call-update) | async-done | bytes 1048592 | tf_op jit(solution)/shard_map/psum | solution.py:76
  478.1 0.0 copy-done.5
  478.1 2.1 fusion.23
  480.1 0.0 all-gather.14.cloned.1.call-update
  480.2 0.0 all-reduce.13.cloned.1.call-start
  480.2 74.6 %all-gather.14.cloned.1.call-done = f32[1,8192,128]{2,1,0:T(8,128)} async-done(((f32[1,1024,128]{2,1,0:T(8,128)}), f32[1,8192,128]{2,1,0:T(8,128)}) %all-gather.14.cloned.1.call-update) | async-done | bytes 4194320 | tf_op jit(solution)/shard_map/all_gather | solution.py:40
  554.8 13.4 %convolution_bitcast_fusion = f32[1024,128]{0,1:T(8,128)} fusion(f32[1024,2048]{1,0:T(8,128)} %param.17, f32[1,8192,128]{2,1,0:T(8,128)} %all-gather.14.cloned.1.call-done, s32[]{:T(128)S(6)} %select_n.55), kind=kOutput, calls=%fused_computation.8 | convolution fusion | flops 3221225472 | bytes 9961476 | tf_op jit(solution)/shard_map/src,sck->srk/dot_general | solution.py:10
  568.3 0.0 all-reduce.13.cloned.1.call-update
  568.3 1.0 copy.38
  569.3 1.0 copy.39
  570.3 29.6 %all-reduce.13.cloned.1.call-done = f32[1024,128]{0,1:T(8,128)} async-done(((f32[1024,128]{0,1:T(8,128)}), f32[1024,128]{0,1:T(8,128)}) %all-reduce.13.cloned.1.call-update) | async-done | bytes 524304 | tf_op jit(solution)/shard_map/psum | solution.py:46
  599.9 2.0 copy.40
  601.9 0.0 copy-done.1
  (16 shorter events, 0.1 us)
Async XLA Ops:
  7.2 81.2 %copy-start = (f32[4,256,512]{2,1,0:T(8,128)S(1)}, f32[4,256,512]{2,1,0:T(8,128)}, u32[]{:S(2)}) copy-start(f32[4,256,512]{2,1,0:T(8,128)} %param.15) | copy-start | bytes 6291460
  7.2 117.0 %copy-start.6 = (s32[4,32,16]{1,2,0:T(8,128)S(1)}, s32[4,32,16]{1,2,0:T(8,128)}, u32[]{:S(2)}) copy-start(s32[4,32,16]{1,2,0:T(8,128)} %param.21) | copy-start | bytes 24580
  7.2 81.2 %all-gather.6.cloned.1.call-start = ((), (), s32[]{:S(2)}) async-start(), calls=%async_computation | async-start | bytes 4718592 | tf_op jit(solution)/shard_map/all_gather | solution.py:40
  9.4 114.7 %all-reduce.7.cloned.1.call-start = ((), (), s32[]{:S(2)}) async-start(), calls=%async_computation.1 | async-start | bytes 1048576 | tf_op jit(solution)/shard_map/psum | solution.py:46
  92.6 108.6 %all-gather.8.cloned.1.call-start = ((), (), s32[]{:S(2)}) async-start(), calls=%async_computation.2 | async-start | bytes 4718592 | tf_op jit(solution)/shard_map/all_gather | solution.py:40
  124.1 117.1 %all-reduce.9.cloned.1.call-start = ((), (), s32[]{:S(2)}) async-start(), calls=%async_computation.3 | async-start | bytes 1048576 | tf_op jit(solution)/shard_map/psum | solution.py:72
  127.1 82.7 %copy-start.4 = (f32[2,512,128]{2,1,0:T(8,128)S(1)}, f32[2,512,128]{2,1,0:T(8,128)}, u32[]{:S(2)}) copy-start(f32[2,512,128]{2,1,0:T(8,128)} %param.13) | copy-start | bytes 1572868
  209.7 107.5 %all-gather.10.cloned.1.call-start = ((), (), s32[]{:S(2)}) async-start(), calls=%async_computation.4 | async-start | bytes 4718592 | tf_op jit(solution)/shard_map/all_gather | solution.py:40
  210.0 146.8 %copy-start.7 = (s32[2,64,32]{1,2,0:T(8,128)S(1)}, s32[2,64,32]{1,2,0:T(8,128)}, u32[]{:S(2)}) copy-start(s32[2,64,32]{1,2,0:T(8,128)} %param.23) | copy-start | bytes 49156
  210.0 146.8 %copy-start.8 = (s32[4,64,16]{1,2,0:T(8,128)S(1)}, s32[4,64,16]{1,2,0:T(8,128)}, u32[]{:S(2)}) copy-start(s32[4,64,16]{1,2,0:T(8,128)} %param.22) | copy-start | bytes 49156
  243.2 113.4 %all-reduce.11.cloned.1.call-start = ((), (), s32[]{:S(2)}) async-start(), calls=%async_computation.5 | async-start | bytes 1048576 | tf_op jit(solution)/shard_map/psum | solution.py:46
  325.0 107.2 %all-gather.12.cloned.1.call-start = ((), (), s32[]{:S(2)}) async-start(), calls=%async_computation.6 | async-start | bytes 4718592 | tf_op jit(solution)/shard_map/all_gather | solution.py:40
  356.6 121.5 %all-reduce.15.cloned.1.call-start = ((), (), s32[]{:S(2)}) async-start(), calls=%async_computation.9 | async-start | bytes 2097152 | tf_op jit(solution)/shard_map/psum | solution.py:76
  357.3 5.8 slice-start
  358.6 4.6 slice-start.1
  371.9 106.2 %copy-start.5 = (f32[1024,128]{1,0:T(8,128)S(1)}, f32[1024,128]{1,0:T(8,128)}, u32[]{:S(2)}) copy-start(f32[1024,128]{1,0:T(8,128)} %param.14) | copy-start | bytes 1572868
  443.5 111.4 %all-gather.14.cloned.1.call-start = ((), (), s32[]{:S(2)}) async-start(), calls=%async_computation.7 | async-start | bytes 4718592 | tf_op jit(solution)/shard_map/all_gather | solution.py:40
  480.2 119.7 %all-reduce.13.cloned.1.call-start = ((), (), s32[]{:S(2)}) async-start(), calls=%async_computation.8 | async-start | bytes 1048576 | tf_op jit(solution)/shard_map/psum | solution.py:46
  480.2 88.1 %copy-start.2 = (f32[4,256,128]{1,2,0:T(8,128)S(1)}, f32[4,256,128]{1,2,0:T(8,128)}, u32[]{:S(2)}) copy-start(f32[4,256,128]{1,2,0:T(8,128)} %all-reduce.7.cloned.1.call-done) | copy-start | bytes 1572868
  480.2 89.1 %copy-start.3 = (f32[2,512,128]{1,2,0:T(8,128)S(1)}, f32[2,512,128]{1,2,0:T(8,128)}, u32[]{:S(2)}) copy-start(f32[2,512,128]{1,2,0:T(8,128)} %all-reduce.11.cloned.1.call-done) | copy-start | bytes 1572868
  554.8 47.1 %copy-start.1 = (f32[4,256,512]{2,1,0:T(8,128)S(1)}, f32[4,256,512]{2,1,0:T(8,128)}, u32[]{:S(2)}) copy-start(f32[4,256,512]{2,1,0:T(8,128)} %param.15) | copy-start | bytes 6291460
Sparse Core Ops, SparseCore 0:
  10.6 77.7 all-gather.5
  92.8 31.3 all-reduce.6
  126.2 75.0 all-gather.7
  209.9 31.3 all-reduce.8
  243.9 73.3 all-gather.9
  325.1 31.4 all-reduce.10
  358.8 73.3 all-gather.11
  443.6 34.4 all-reduce.14
  481.0 73.8 all-gather.13
  568.4 31.4 all-reduce.12
where the time goes:
time: 609 us
  waiting for transfers between devices  520 us (85%)
  matrix products  61.8 us (10%)
  between operations  14.4 us (2%)
  local copies, waits for them, and re-layouts  7.45 us (1%)
    all_gather x5, waiting for transfers between devices, fetch_columns(): gathered = lax.all_gather(block, 'rows', axis=1, tiled=True)  362 us
    psum x3, waiting for transfers between devices, solve_block(): solved = lax.psum(partial_value, 'cols')  92.6 us
    dot_general x6, matrix products, product(): jnp.einsum('src,sck->srk', matrix, vector, precision=lax.Precision.HIGHES...  52.8 us
    psum x1, waiting for transfers between devices, body(): resid_root = right_root[None] - root_summed - lax.psum(root_more, 'cols')  34.5 us
    psum x1, waiting for transfers between devices, body(): mid_summed, root_summed = lax.psum((mid_part, root_part), 'cols')  31.2 us
  transfers between devices with their start and end apart: 10, of which 10 were waited for; matrix products, arithmetic and copies ran while one was open for 3% of the time, Pallas kernels for 0%

commit v1 on v0

--- a/solution.py
+++ b/solution.py
@@ -37,7 +37,17 @@
 
 
 def fetch_columns(block):
-    gathered = lax.all_gather(block, "rows", axis=1, tiled=True)
+    lanes = lax.psum(1, "rows")
+    shaped = block
+    reply = sorted(((j0, (j0 + 1) % lanes) for j0 in range(lanes)))
+    shelf = [shaped]
+    for dev_j in [*range(1, lanes)]:
+        shaped = lax.ppermute(shaped, "rows", reply)
+        shelf.insert(0, shaped)
+    top = jnp.concatenate(shelf, axis=1)
+    mid_arr = lax.axis_index("rows")
+    tmp = mid_arr + 1
+    gathered = jnp.roll(top, tmp * block.shape[1], axis=1)
     return own_columns(gathered)
 
 

time: 609 us -> 725 us (1.19); the launches traced: 609 us -> 716 us
  waiting for transfers between devices: 520 us -> 609 us
  local copies, waits for them, and re-layouts: 7.45 us -> 35.9 us
  matrix products: 61.8 us -> 43.7 us
  starting transfers between devices: 0.59 us -> 10.1 us
    ppermute x0 -> x35, waiting for transfers between devices: none -> 453 us  [fetch_columns(): shaped = lax.ppermute(shaped, 'rows', reply)]
    all_gather x5 -> x0, waiting for transfers between devices: 362 us -> none  [fetch_columns(): gathered = lax.all_gather(block, 'rows', axis=1, tiled=True)]
    unnamed x27 -> x112, local copies, waits for them, and re-layouts: 6.46 us -> 34.7 us
    dot_general x6, matrix products: 52.8 us -> 39.9 us  [product(): jnp.einsum('src,sck->srk', matrix, vector, precision=lax.Precision.HIGHES...]
    ppermute x0 -> x35, starting transfers between devices: none -> 9.94 us  [fetch_columns(): shaped = lax.ppermute(shaped, 'rows', reply)]
  transfers between devices with their start and end apart: 10 -> 40, of which waited for: 10 -> 40; matrix products, arithmetic and copies ran while one was open for 3% -> 2% of each run, Pallas kernels for 0% -> 0%
where the time goes in v1:
time: 725 us; the launch traced here: 716 us
  waiting for transfers between devices  609 us (84%)
  matrix products  43.7 us (6%)
  local copies, waits for them, and re-layouts  35.9 us (5%)
  between operations  14.8 us (2%)
  starting transfers between devices  10.1 us (1%)
    ppermute x35, waiting for transfers between devices, fetch_columns(): shaped = lax.ppermute(shaped, 'rows', reply)  453 us
    psum x3, waiting for transfers between devices, solve_block(): solved = lax.psum(partial_value, 'cols')  89.5 us
    dot_general x6, matrix products, product(): jnp.einsum('src,sck->srk', matrix, vector, precision=lax.Precision.HIGHES...  39.9 us
    psum x1, waiting for transfers between devices, body(): resid_root = right_root[None] - root_summed - lax.psum(root_more, 'cols')  35.9 us
    unnamed x112, local copies, waits for them, and re-layouts  34.7 us
    psum x1, waiting for transfers between devices, body(): mid_summed, root_summed = lax.psum((mid_part, root_part), 'cols')  30.5 us
  transfers between devices with their start and end apart: 40, of which 40 were waited for; matrix products, arithmetic and copies ran while one was open for 2% of the time, Pallas kernels for 0%

profile of v1, /device:TPU:0, one launch (start us, length us, event | category | flops | bytes accessed | tf_op | source)
XLA Modules:
  0.0 716.4 jit_solution(5162113084156501975)
XLA Ops:
  7.2 1.4 copy.34
  8.6 3.0 collective-permute-start
  11.6 15.0 %collective-permute-done = f32[4,256,128]{1,2,0:T(8,128)S(1)} collective-permute-done((f32[4,256,128]{1,2,0:T(8,128)S(1)}, f32[4,256,128]{1,2,0:T(8,128)S(1)}, u32[]{:S(2)}, u32[]{:S(2)}) %collective-permute-start) | collective-permute-done | bytes 524320 | tf_op jit(solution)/shard_map/ppermute | solution.py:45
  26.6 15.8 %collective-permute-done.1 = f32[4,256,128]{1,2,0:T(8,128)S(1)} collective-permute-done((f32[4,256,128]{1,2,0:T(8,128)S(1)}, f32[4,256,128]{1,2,0:T(8,128)S(1)}, u32[]{:S(2)}, u32[]{:S(2)}) %collective-permute-start.1) | collective-permute-done | bytes 524320 | tf_op jit(solution)/shard_map/ppermute | solution.py:45
  43.2 14.9 %collective-permute-done.2 = f32[4,256,128]{1,2,0:T(8,128)S(1)} collective-permute-done((f32[4,256,128]{1,2,0:T(8,128)S(1)}, f32[4,256,128]{1,2,0:T(8,128)S(1)}, u32[]{:S(2)}, u32[]{:S(2)}) %collective-permute-start.2) | collective-permute-done | bytes 524320 | tf_op jit(solution)/shard_map/ppermute | solution.py:45
  58.9 14.0 %collective-permute-done.3 = f32[4,256,128]{1,2,0:T(8,128)S(1)} collective-permute-done((f32[4,256,128]{1,2,0:T(8,128)S(1)}, f32[4,256,128]{1,2,0:T(8,128)S(1)}, u32[]{:S(2)}, u32[]{:S(2)}) %collective-permute-start.3) | collective-permute-done | bytes 524320 | tf_op jit(solution)/shard_map/ppermute | solution.py:45
  73.6 13.0 %collective-permute-done.4 = f32[4,256,128]{1,2,0:T(8,128)S(1)} collective-permute-done((f32[4,256,128]{1,2,0:T(8,128)S(1)}, f32[4,256,128]{1,2,0:T(8,128)S(1)}, u32[]{:S(2)}, u32[]{:S(2)}) %collective-permute-start.4) | collective-permute-done | bytes 524320 | tf_op jit(solution)/shard_map/ppermute | solution.py:45
  87.5 12.2 %collective-permute-done.5 = f32[4,256,128]{1,2,0:T(8,128)} collective-permute-done((f32[4,256,128]{1,2,0:T(8,128)S(1)}, f32[4,256,128]{1,2,0:T(8,128)}, u32[]{:S(2)}, u32[]{:S(2)}) %collective-permute-start.5) | collective-permute-done | bytes 524320 | tf_op jit(solution)/shard_map/ppermute | solution.py:45
  99.7 12.2 %collective-permute-done.6 = f32[4,256,128]{1,2,0:T(8,128)} collective-permute-done((f32[4,256,128]{1,2,0:T(8,128)}, f32[4,256,128]{1,2,0:T(8,128)}, u32[]{:S(2)}, u32[]{:S(2)}) %collective-permute-start.6) | collective-permute-done | bytes 524320 | tf_op jit(solution)/shard_map/ppermute | solution.py:45
  113.0 1.1 constant_dynamic-update-slice_fusion.6
  116.7 3.2 convolution_bitcast_fusion.1
  120.0 30.4 %all-reduce.7.cloned.1.call-done = f32[4,256,128]{1,2,0:T(8,128)} async-done(((f32[4,256,128]{1,2,0:T(8,128)}), f32[4,256,128]{1,2,0:T(8,128)}) %all-reduce.7.cloned.1.call-update) | async-done | bytes 524304 | tf_op jit(solution)/shard_map/psum | solution.py:56
  150.4 1.5 collective-permute-start.7
  151.9 14.0 %collective-permute-done.7 = f32[4,256,128]{1,2,0:T(8,128)S(1)} collective-permute-done((f32[4,256,128]{1,2,0:T(8,128)}, f32[4,256,128]{1,2,0:T(8,128)S(1)}, u32[]{:S(2)}, u32[]{:S(2)}) %collective-permute-start.7) | collective-permute-done | bytes 524320 | tf_op jit(solution)/shard_map/ppermute | solution.py:45
  165.8 14.3 %collective-permute-done.8 = f32[4,256,128]{1,2,0:T(8,128)S(1)} collective-permute-done((f32[4,256,128]{1,2,0:T(8,128)S(1)}, f32[4,256,128]{1,2,0:T(8,128)S(1)}, u32[]{:S(2)}, u32[]{:S(2)}) %collective-permute-start.8) | collective-permute-done | bytes 524320 | tf_op jit(solution)/shard_map/ppermute | solution.py:45
  180.1 13.4 %collective-permute-done.9 = f32[4,256,128]{1,2,0:T(8,128)S(1)} collective-permute-done((f32[4,256,128]{1,2,0:T(8,128)S(1)}, f32[4,256,128]{1,2,0:T(8,128)S(1)}, u32[]{:S(2)}, u32[]{:S(2)}) %collective-permute-start.9) | collective-permute-done | bytes 524320 | tf_op jit(solution)/shard_map/ppermute | solution.py:45
  193.5 12.5 %collective-permute-done.10 = f32[4,256,128]{1,2,0:T(8,128)S(1)} collective-permute-done((f32[4,256,128]{1,2,0:T(8,128)S(1)}, f32[4,256,128]{1,2,0:T(8,128)S(1)}, u32[]{:S(2)}, u32[]{:S(2)}) %collective-permute-start.10) | collective-permute-done | bytes 524320 | tf_op jit(solution)/shard_map/ppermute | solution.py:45
  206.0 12.6 %collective-permute-done.11 = f32[4,256,128]{1,2,0:T(8,128)S(1)} collective-permute-done((f32[4,256,128]{1,2,0:T(8,128)S(1)}, f32[4,256,128]{1,2,0:T(8,128)S(1)}, u32[]{:S(2)}, u32[]{:S(2)}) %collective-permute-start.11) | collective-permute-done | bytes 524320 | tf_op jit(solution)/shard_map/ppermute | solution.py:45
  218.7 13.5 %collective-permute-done.12 = f32[4,256,128]{1,2,0:T(8,128)} collective-permute-done((f32[4,256,128]{1,2,0:T(8,128)S(1)}, f32[4,256,128]{1,2,0:T(8,128)}, u32[]{:S(2)}, u32[]{:S(2)}) %collective-permute-start.12) | collective-permute-done | bytes 524320 | tf_op jit(solution)/shard_map/ppermute | solution.py:45
  233.1 11.2 %collective-permute-done.13 = f32[4,256,128]{1,2,0:T(8,128)S(1)} collective-permute-done((f32[4,256,128]{1,2,0:T(8,128)}, f32[4,256,128]{1,2,0:T(8,128)S(1)}, u32[]{:S(2)}, u32[]{:S(2)}) %collective-permute-start.13) | collective-permute-done | bytes 524320 | tf_op jit(solution)/shard_map/ppermute | solution.py:45
  246.9 2.0 copy-done.2
  248.9 4.1 bitcast_reduce_fusion
  254.3 30.5 %all-reduce.9.cloned.1.call-done = f32[2,512,128]{1,2,0:T(8,128)} async-done(((f32[2,512,128]{1,2,0:T(8,128)}), f32[2,512,128]{1,2,0:T(8,128)}) %all-reduce.9.cloned.1.call-update) | async-done | bytes 524304 | tf_op jit(solution)/shard_map/psum | solution.py:82
  284.8 1.1 sub.45
  285.9 1.5 collective-permute-start.14
  287.4 13.8 %collective-permute-done.14 = f32[2,512,128]{1,2,0:T(8,128)S(1)} collective-permute-done((f32[2,512,128]{1,2,0:T(8,128)S(1)}, f32[2,512,128]{1,2,0:T(8,128)S(1)}, u32[]{:S(2)}, u32[]{:S(2)}) %collective-permute-start.14) | collective-permute-done | bytes 524320 | tf_op jit(solution)/shard_map/ppermute | solution.py:45
  301.2 14.3 %collective-permute-done.15 = f32[2,512,128]{1,2,0:T(8,128)S(1)} collective-permute-done((f32[2,512,128]{1,2,0:T(8,128)S(1)}, f32[2,512,128]{1,2,0:T(8,128)S(1)}, u32[]{:S(2)}, u32[]{:S(2)}) %collective-permute-start.15) | collective-permute-done | bytes 524320 | tf_op jit(solution)/shard_map/ppermute | solution.py:45
  315.5 13.4 %collective-permute-done.16 = f32[2,512,128]{1,2,0:T(8,128)S(1)} collective-permute-done((f32[2,512,128]{1,2,0:T(8,128)S(1)}, f32[2,512,128]{1,2,0:T(8,128)S(1)}, u32[]{:S(2)}, u32[]{:S(2)}) %collective-permute-start.16) | collective-permute-done | bytes 524320 | tf_op jit(solution)/shard_map/ppermute | solution.py:45
  328.9 12.5 %collective-permute-done.17 = f32[2,512,128]{1,2,0:T(8,128)S(1)} collective-permute-done((f32[2,512,128]{1,2,0:T(8,128)S(1)}, f32[2,512,128]{1,2,0:T(8,128)S(1)}, u32[]{:S(2)}, u32[]{:S(2)}) %collective-permute-start.17) | collective-permute-done | bytes 524320 | tf_op jit(solution)/shard_map/ppermute | solution.py:45
  341.3 11.9 %collective-permute-done.18 = f32[2,512,128]{1,2,0:T(8,128)S(1)} collective-permute-done((f32[2,512,128]{1,2,0:T(8,128)S(1)}, f32[2,512,128]{1,2,0:T(8,128)S(1)}, u32[]{:S(2)}, u32[]{:S(2)}) %collective-permute-start.18) | collective-permute-done | bytes 524320 | tf_op jit(solution)/shard_map/ppermute | solution.py:45
  354.0 13.1 %collective-permute-done.19 = f32[2,512,128]{1,2,0:T(8,128)} collective-permute-done((f32[2,512,128]{1,2,0:T(8,128)S(1)}, f32[2,512,128]{1,2,0:T(8,128)}, u32[]{:S(2)}, u32[]{:S(2)}) %collective-permute-start.19) | collective-permute-done | bytes 524320 | tf_op jit(solution)/shard_map/ppermute | solution.py:45
  367.6 12.1 %collective-permute-done.20 = f32[2,512,128]{1,2,0:T(8,128)} collective-permute-done((f32[2,512,128]{1,2,0:T(8,128)}, f32[2,512,128]{1,2,0:T(8,128)}, u32[]{:S(2)}, u32[]{:S(2)}) %collective-permute-start.20) | collective-permute-done | bytes 524320 | tf_op jit(solution)/shard_map/ppermute | solution.py:45
  383.3 5.1 convolution_bitcast_fusion.2
  388.4 31.4 %all-reduce.11.cloned.1.call-done = f32[2,512,128]{1,2,0:T(8,128)} async-done(((f32[2,512,128]{1,2,0:T(8,128)}), f32[2,512,128]{1,2,0:T(8,128)}) %all-reduce.11.cloned.1.call-update) | async-done | bytes 524304 | tf_op jit(solution)/shard_map/psum | solution.py:56
  419.9 1.5 collective-permute-start.21
  421.3 14.0 %collective-permute-done.21 = f32[2,512,128]{1,2,0:T(8,128)S(1)} collective-permute-done((f32[2,512,128]{1,2,0:T(8,128)}, f32[2,512,128]{1,2,0:T(8,128)S(1)}, u32[]{:S(2)}, u32[]{:S(2)}) %collective-permute-start.21) | collective-permute-done | bytes 524320 | tf_op jit(solution)/shard_map/ppermute | solution.py:45
  435.3 14.3 %collective-permute-done.22 = f32[2,512,128]{1,2,0:T(8,128)S(1)} collective-permute-done((f32[2,512,128]{1,2,0:T(8,128)S(1)}, f32[2,512,128]{1,2,0:T(8,128)S(1)}, u32[]{:S(2)}, u32[]{:S(2)}) %collective-permute-start.22) | collective-permute-done | bytes 524320 | tf_op jit(solution)/shard_map/ppermute | solution.py:45
  449.6 13.4 %collective-permute-done.23 = f32[2,512,128]{1,2,0:T(8,128)S(1)} collective-permute-done((f32[2,512,128]{1,2,0:T(8,128)S(1)}, f32[2,512,128]{1,2,0:T(8,128)S(1)}, u32[]{:S(2)}, u32[]{:S(2)}) %collective-permute-start.23) | collective-permute-done | bytes 524320 | tf_op jit(solution)/shard_map/ppermute | solution.py:45
  463.2 12.2 %collective-permute-done.24 = f32[2,512,128]{1,2,0:T(8,128)S(1)} collective-permute-done((f32[2,512,128]{1,2,0:T(8,128)S(1)}, f32[2,512,128]{1,2,0:T(8,128)S(1)}, u32[]{:S(2)}, u32[]{:S(2)}) %collective-permute-start.24) | collective-permute-done | bytes 524320 | tf_op jit(solution)/shard_map/ppermute | solution.py:45
  475.7 1.3 fusion.33
  476.9 11.2 %collective-permute-done.25 = f32[2,512,128]{1,2,0:T(8,128)S(1)} collective-permute-done((f32[2,512,128]{1,2,0:T(8,128)S(1)}, f32[2,512,128]{1,2,0:T(8,128)S(1)}, u32[]{:S(2)}, u32[]{:S(2)}) %collective-permute-start.25) | collective-permute-done | bytes 524320 | tf_op jit(solution)/shard_map/ppermute | solution.py:45
  488.1 1.3 fusion.27
  489.5 12.0 %collective-permute-done.26 = f32[2,512,128]{1,2,0:T(8,128)} collective-permute-done((f32[2,512,128]{1,2,0:T(8,128)S(1)}, f32[2,512,128]{1,2,0:T(8,128)}, u32[]{:S(2)}, u32[]{:S(2)}) %collective-permute-start.26) | collective-permute-done | bytes 524320 | tf_op jit(solution)/shard_map/ppermute | solution.py:45
  501.7 10.2 %fusion.6 = f32[1,1024,128]{2,1,0:T(8,128)} fusion(f32[4,1024,512]{2,1,0:T(8,128)} %param.23, f32[4,1024,512]{2,1,0:T(8,128)S(1)} %fusion.33, s32[]{:T(128)S(6)} %add.152, f32[4,2048,128]{1,2,0:T(8,128)S(1)} %copy-done.3), kind=kOutput, calls=%fused_computation.14 | convolution fusion | flops 3223584768 | bytes 21495812 | tf_op jit(solution)/shard_map/src,sck->srk/dot_general | solution.py:10
  511.8 2.0 collective-permute-done.27
  517.3 7.6 %fusion.9 = f32[1,1024,128]{2,1,0:T(8,128)} fusion(f32[2,1024,1024]{2,1,0:T(8,128)S(1)} %bitcast.58, f32[2,1024,1024]{2,1,0:T(8,128)S(1)} %fusion.27, s32[]{:T(128)S(6)} %add.158, f32[2,4096,128]{1,2,0:T(8,128)S(1)} %constant_dynamic-update-slice_fusion.24), kind=kOutput, calls=%fused_computation.15 | convolution fusion | flops 3223584768 | bytes 21495812 | tf_op jit(solution)/shard_map/src,sck->srk/dot_general | solution.py:10
  525.0 35.9 %all-reduce.15.cloned.1.call-done = (f32[1,1024,128]{2,1,0:T(8,128)}, f32[1,1024,128]{2,1,0:T(8,128)}) async-done(((f32[1,1024,128]{2,1,0:T(8,128)}, f32[1,1024,128]{2,1,0:T(8,128)}), (f32[1,1024,128]{2,1,0:T(8,128)}, f32[1,1024,128]{2,1,0:T(8,128)})) %all-reduce.15.cloned.1.call-update) | async-done | bytes 1048592 | tf_op jit(solution)/shard_map/psum | solution.py:86
  560.9 1.3 fusion.21
  562.2 1.5 collective-permute-start.28
  563.7 14.7 %collective-permute-done.28 = f32[1,1024,128]{2,1,0:T(8,128)S(1)} collective-permute-done((f32[1,1024,128]{2,1,0:T(8,128)S(1)}, f32[1,1024,128]{2,1,0:T(8,128)S(1)}, u32[]{:S(2)}, u32[]{:S(2)}) %collective-permute-start.28) | collective-permute-done | bytes 524320 | tf_op jit(solution)/shard_map/ppermute | solution.py:45
  578.4 15.3 %collective-permute-done.29 = f32[1,1024,128]{2,1,0:T(8,128)S(1)} collective-permute-done((f32[1,1024,128]{2,1,0:T(8,128)S(1)}, f32[1,1024,128]{2,1,0:T(8,128)S(1)}, u32[]{:S(2)}, u32[]{:S(2)}) %collective-permute-start.29) | collective-permute-done | bytes 524320 | tf_op jit(solution)/shard_map/ppermute | solution.py:45
  593.7 14.4 %collective-permute-done.30 = f32[1,1024,128]{2,1,0:T(8,128)S(1)} collective-permute-done((f32[1,1024,128]{2,1,0:T(8,128)S(1)}, f32[1,1024,128]{2,1,0:T(8,128)S(1)}, u32[]{:S(2)}, u32[]{:S(2)}) %collective-permute-start.30) | collective-permute-done | bytes 524320 | tf_op jit(solution)/shard_map/ppermute | solution.py:45
  608.1 13.4 %collective-permute-done.31 = f32[1,1024,128]{2,1,0:T(8,128)S(1)} collective-permute-done((f32[1,1024,128]{2,1,0:T(8,128)S(1)}, f32[1,1024,128]{2,1,0:T(8,128)S(1)}, u32[]{:S(2)}, u32[]{:S(2)}) %collective-permute-start.31) | collective-permute-done | bytes 524320 | tf_op jit(solution)/shard_map/ppermute | solution.py:45
  622.3 12.5 %collective-permute-done.32 = f32[1,1024,128]{2,1,0:T(8,128)S(1)} collective-permute-done((f32[1,1024,128]{2,1,0:T(8,128)S(1)}, f32[1,1024,128]{2,1,0:T(8,128)S(1)}, u32[]{:S(2)}, u32[]{:S(2)}) %collective-permute-start.32) | collective-permute-done | bytes 524320 | tf_op jit(solution)/shard_map/ppermute | solution.py:45
  635.9 12.4 %collective-permute-done.33 = f32[1,1024,128]{2,1,0:T(8,128)} collective-permute-done((f32[1,1024,128]{2,1,0:T(8,128)S(1)}, f32[1,1024,128]{2,1,0:T(8,128)}, u32[]{:S(2)}, u32[]{:S(2)}) %collective-permute-start.33) | collective-permute-done | bytes 524320 | tf_op jit(solution)/shard_map/ppermute | solution.py:45
  648.3 12.2 %collective-permute-done.34 = f32[1,1024,128]{2,1,0:T(8,128)} collective-permute-done((f32[1,1024,128]{2,1,0:T(8,128)}, f32[1,1024,128]{2,1,0:T(8,128)}, u32[]{:S(2)}, u32[]{:S(2)}) %collective-permute-start.34) | collective-permute-done | bytes 524320 | tf_op jit(solution)/shard_map/ppermute | solution.py:45
  661.5 1.2 constant_dynamic-update-slice_fusion.46
  662.8 1.3 constant_dynamic-update-slice_fusion.45
  664.1 1.1 constant_dynamic-update-slice_fusion.44
  665.4 1.2 constant_dynamic-update-slice_fusion.39
  666.6 1.3 constant_dynamic-update-slice_fusion.38
  668.2 9.6 %convolution_bitcast_fusion = f32[1024,128]{0,1:T(8,128)} fusion(f32[1024,2048]{1,0:T(8,128)S(1)} %bitcast.56, f32[1,16384,128]{2,1,0:T(8,128)S(1)} %constant_dynamic-update-slice_fusion.32, s32[]{:T(128)S(6)} %dynamic_slice.30), kind=kOutput, calls=%fused_computation.16 | convolution fusion | flops 3221225472 | bytes 9961476 | tf_op jit(solution)/shard_map/src,sck->srk/dot_general | solution.py:10
  679.9 27.7 %all-reduce.13.cloned.1.call-done = f32[1024,128]{0,1:T(8,128)} async-done(((f32[1024,128]{0,1:T(8,128)}), f32[1024,128]{0,1:T(8,128)}) %all-reduce.13.cloned.1.call-update) | async-done | bytes 524304 | tf_op jit(solution)/shard_map/psum | solution.py:56
  707.6 2.0 copy.43
  (162 shorter events, 25.8 us)
Async XLA Ops:
  7.2 109.5 %copy-start = (f32[4,256,512]{2,1,0:T(8,128)S(1)}, f32[4,256,512]{2,1,0:T(8,128)}, u32[]{:S(2)}) copy-start(f32[4,256,512]{2,1,0:T(8,128)} %param.19) | copy-start | bytes 6291460
  7.2 143.2 %all-reduce.7.cloned.1.call-start = ((), (), s32[]{:S(2)}) async-start(), calls=%async_computation | async-start | bytes 1048576 | tf_op jit(solution)/shard_map/psum | solution.py:56
  8.6 18.0 %collective-permute-start = (f32[4,256,128]{1,2,0:T(8,128)S(1)}, f32[4,256,128]{1,2,0:T(8,128)S(1)}, u32[]{:S(2)}, u32[]{:S(2)}) collective-permute-start(f32[4,256,128]{1,2,0:T(8,128)S(1)} %copy.34), channel_id=1, source_target_pairs={{0,4},{4,8},{8,12},{12,16},{16,20},{20,24},{24,28},{28,0},{1,5},{5... | collective-permute-start | bytes 1572872 | tf_op jit(solution)/shard_map/ppermute | solution.py:45
  26.6 15.8 %collective-permute-start.1 = (f32[4,256,128]{1,2,0:T(8,128)S(1)}, f32[4,256,128]{1,2,0:T(8,128)S(1)}, u32[]{:S(2)}, u32[]{:S(2)}) collective-permute-start(f32[4,256,128]{1,2,0:T(8,128)S(1)} %collective-permute-done), channel_id=1, source_target_pairs={{0,4},{4,8},{8,12},{12,16},{16,20},{20,24},{24,28},{28,0},{1,5},{5... | collective-permute-start | bytes 1572872 | tf_op jit(solution)/shard_map/ppermute | solution.py:45
  43.2 14.9 %collective-permute-start.2 = (f32[4,256,128]{1,2,0:T(8,128)S(1)}, f32[4,256,128]{1,2,0:T(8,128)S(1)}, u32[]{:S(2)}, u32[]{:S(2)}) collective-permute-start(f32[4,256,128]{1,2,0:T(8,128)S(1)} %collective-permute-done.1), channel_id=1, source_target_pairs={{0,4},{4,8},{8,12},{12,16},{16,20},{20,24},{24,28},{28,0},{1,5},{5... | collective-permute-start | bytes 1572872 | tf_op jit(solution)/shard_map/ppermute | solution.py:45
  58.9 14.0 %collective-permute-start.3 = (f32[4,256,128]{1,2,0:T(8,128)S(1)}, f32[4,256,128]{1,2,0:T(8,128)S(1)}, u32[]{:S(2)}, u32[]{:S(2)}) collective-permute-start(f32[4,256,128]{1,2,0:T(8,128)S(1)} %collective-permute-done.2), channel_id=1, source_target_pairs={{0,4},{4,8},{8,12},{12,16},{16,20},{20,24},{24,28},{28,0},{1,5},{5... | collective-permute-start | bytes 1572872 | tf_op jit(solution)/shard_map/ppermute | solution.py:45
  73.6 13.0 %collective-permute-start.4 = (f32[4,256,128]{1,2,0:T(8,128)S(1)}, f32[4,256,128]{1,2,0:T(8,128)S(1)}, u32[]{:S(2)}, u32[]{:S(2)}) collective-permute-start(f32[4,256,128]{1,2,0:T(8,128)S(1)} %collective-permute-done.3), channel_id=1, source_target_pairs={{0,4},{4,8},{8,12},{12,16},{16,20},{20,24},{24,28},{28,0},{1,5},{5... | collective-permute-start | bytes 1572872 | tf_op jit(solution)/shard_map/ppermute | solution.py:45
  87.5 12.2 %collective-permute-start.5 = (f32[4,256,128]{1,2,0:T(8,128)S(1)}, f32[4,256,128]{1,2,0:T(8,128)}, u32[]{:S(2)}, u32[]{:S(2)}) collective-permute-start(f32[4,256,128]{1,2,0:T(8,128)S(1)} %collective-permute-done.4), channel_id=1, source_target_pairs={{0,4},{4,8},{8,12},{12,16},{16,20},{20,24},{24,28},{28,0},{1,5},{5... | collective-permute-start | bytes 1572872 | tf_op jit(solution)/shard_map/ppermute | solution.py:45
  99.7 12.2 %collective-permute-start.6 = (f32[4,256,128]{1,2,0:T(8,128)}, f32[4,256,128]{1,2,0:T(8,128)}, u32[]{:S(2)}, u32[]{:S(2)}) collective-permute-start(f32[4,256,128]{1,2,0:T(8,128)} %collective-permute-done.5), channel_id=1, source_target_pairs={{0,4},{4,8},{8,12},{12,16},{16,20},{20,24},{24,28},{28,0},{1,5},{5... | collective-permute-start | bytes 1572872 | tf_op jit(solution)/shard_map/ppermute | solution.py:45
  99.7 16.7 %copy-start.16 = (f32[4,256,128]{1,2,0:T(8,128)S(1)}, f32[4,256,128]{1,2,0:T(8,128)}, u32[]{:S(2)}) copy-start(f32[4,256,128]{1,2,0:T(8,128)} %copy-done.15) | copy-start | bytes 1572868
  99.7 16.7 %copy-start.14 = (f32[4,256,128]{1,2,0:T(8,128)S(1)}, f32[4,256,128]{1,2,0:T(8,128)}, u32[]{:S(2)}) copy-start(f32[4,256,128]{1,2,0:T(8,128)} %copy-done.13) | copy-start | bytes 1572868
  116.6 102.1 %copy-start.25 = (s32[4,32,16]{1,2,0:T(8,128)S(1)}, s32[4,32,16]{1,2,0:T(8,128)}, u32[]{:S(2)}) copy-start(s32[4,32,16]{1,2,0:T(8,128)} %param.25) | copy-start | bytes 24580
  119.9 164.8 %all-reduce.9.cloned.1.call-start = ((), (), s32[]{:S(2)}) async-start(), calls=%async_computation.1 | async-start | bytes 1048576 | tf_op jit(solution)/shard_map/psum | solution.py:82
  150.4 15.4 %collective-permute-start.7 = (f32[4,256,128]{1,2,0:T(8,128)}, f32[4,256,128]{1,2,0:T(8,128)S(1)}, u32[]{:S(2)}, u32[]{:S(2)}) collective-permute-start(f32[4,256,128]{1,2,0:T(8,128)} %all-reduce.7.cloned.1.call-done), channel_id=1, source_target_pairs={{0,4},{4,8},{8,12},{12,16},{16,20},{20,24},{24,28},{28,0},{1,5},{5... | collective-permute-start | bytes 1572872 | tf_op jit(solution)/shard_map/ppermute | solution.py:45
  165.8 14.3 %collective-permute-start.8 = (f32[4,256,128]{1,2,0:T(8,128)S(1)}, f32[4,256,128]{1,2,0:T(8,128)S(1)}, u32[]{:S(2)}, u32[]{:S(2)}) collective-permute-start(f32[4,256,128]{1,2,0:T(8,128)S(1)} %collective-permute-done.7), channel_id=1, source_target_pairs={{0,4},{4,8},{8,12},{12,16},{16,20},{20,24},{24,28},{28,0},{1,5},{5... | collective-permute-start | bytes 1572872 | tf_op jit(solution)/shard_map/ppermute | solution.py:45
  180.1 13.4 %collective-permute-start.9 = (f32[4,256,128]{1,2,0:T(8,128)S(1)}, f32[4,256,128]{1,2,0:T(8,128)S(1)}, u32[]{:S(2)}, u32[]{:S(2)}) collective-permute-start(f32[4,256,128]{1,2,0:T(8,128)S(1)} %collective-permute-done.8), channel_id=1, source_target_pairs={{0,4},{4,8},{8,12},{12,16},{16,20},{20,24},{24,28},{28,0},{1,5},{5... | collective-permute-start | bytes 1572872 | tf_op jit(solution)/shard_map/ppermute | solution.py:45
  193.5 12.5 %collective-permute-start.10 = (f32[4,256,128]{1,2,0:T(8,128)S(1)}, f32[4,256,128]{1,2,0:T(8,128)S(1)}, u32[]{:S(2)}, u32[]{:S(2)}) collective-permute-start(f32[4,256,128]{1,2,0:T(8,128)S(1)} %collective-permute-done.9), channel_id=1, source_target_pairs={{0,4},{4,8},{8,12},{12,16},{16,20},{20,24},{24,28},{28,0},{1,5},{5... | collective-permute-start | bytes 1572872 | tf_op jit(solution)/shard_map/ppermute | solution.py:45
  206.0 12.6 %collective-permute-start.11 = (f32[4,256,128]{1,2,0:T(8,128)S(1)}, f32[4,256,128]{1,2,0:T(8,128)S(1)}, u32[]{:S(2)}, u32[]{:S(2)}) collective-permute-start(f32[4,256,128]{1,2,0:T(8,128)S(1)} %collective-permute-done.10), channel_id=1, source_target_pairs={{0,4},{4,8},{8,12},{12,16},{16,20},{20,24},{24,28},{28,0},{1,5},{5... | collective-permute-start | bytes 1572872 | tf_op jit(solution)/shard_map/ppermute | solution.py:45
  218.6 13.7 %copy-start.23 = (f32[4,256,128]{1,2,0:T(8,128)}, f32[4,256,128]{1,2,0:T(8,128)S(1)}, u32[]{:S(2)}) copy-start(f32[4,256,128]{1,2,0:T(8,128)S(1)} %collective-permute-done.11) | copy-start | bytes 1572868
  218.6 13.5 %collective-permute-start.12 = (f32[4,256,128]{1,2,0:T(8,128)S(1)}, f32[4,256,128]{1,2,0:T(8,128)}, u32[]{:S(2)}, u32[]{:S(2)}) collective-permute-start(f32[4,256,128]{1,2,0:T(8,128)S(1)} %collective-permute-done.11), channel_id=1, source_target_pairs={{0,4},{4,8},{8,12},{12,16},{16,20},{20,24},{24,28},{28,0},{1,5},{5... | collective-permute-start | bytes 1572872 | tf_op jit(solution)/shard_map/ppermute | solution.py:45
  232.2 12.1 %collective-permute-start.13 = (f32[4,256,128]{1,2,0:T(8,128)}, f32[4,256,128]{1,2,0:T(8,128)S(1)}, u32[]{:S(2)}, u32[]{:S(2)}) collective-permute-start(f32[4,256,128]{1,2,0:T(8,128)} %collective-permute-done.12), channel_id=1, source_target_pairs={{0,4},{4,8},{8,12},{12,16},{16,20},{20,24},{24,28},{28,0},{1,5},{5... | collective-permute-start | bytes 1572872 | tf_op jit(solution)/shard_map/ppermute | solution.py:45
  233.1 13.7 %copy-start.6 = (f32[4,256,128]{1,2,0:T(8,128)S(1)}, f32[4,256,128]{1,2,0:T(8,128)}, u32[]{:S(2)}) copy-start(f32[4,256,128]{1,2,0:T(8,128)} %all-reduce.7.cloned.1.call-done) | copy-start | bytes 1572868
  233.1 15.8 %copy-start.4 = (f32[4,512,512]{2,1,0:T(8,128)S(1)}, f32[4,512,512]{2,1,0:T(8,128)}, u32[]{:S(2)}) copy-start(f32[4,512,512]{2,1,0:T(8,128)} %param.22) | copy-start | bytes 12582916
  246.9 2.0 copy-start.2
  248.9 5.2 copy-start.12
  254.0 165.8 %all-reduce.11.cloned.1.call-start = ((), (), s32[]{:S(2)}) async-start(), calls=%async_computation.2 | async-start | bytes 1048576 | tf_op jit(solution)/shard_map/psum | solution.py:56
  285.9 15.3 %collective-permute-start.14 = (f32[2,512,128]{1,2,0:T(8,128)S(1)}, f32[2,512,128]{1,2,0:T(8,128)S(1)}, u32[]{:S(2)}, u32[]{:S(2)}) collective-permute-start(f32[2,512,128]{1,2,0:T(8,128)S(1)} %sub.45), channel_id=1, source_target_pairs={{0,4},{4,8},{8,12},{12,16},{16,20},{20,24},{24,28},{28,0},{1,5},{5... | collective-permute-start | bytes 1572872 | tf_op jit(solution)/shard_map/ppermute | solution.py:45
  301.2 14.3 %collective-permute-start.15 = (f32[2,512,128]{1,2,0:T(8,128)S(1)}, f32[2,512,128]{1,2,0:T(8,128)S(1)}, u32[]{:S(2)}, u32[]{:S(2)}) collective-permute-start(f32[2,512,128]{1,2,0:T(8,128)S(1)} %collective-permute-done.14), channel_id=1, source_target_pairs={{0,4},{4,8},{8,12},{12,16},{16,20},{20,24},{24,28},{28,0},{1,5},{5... | collective-permute-start | bytes 1572872 | tf_op jit(solution)/shard_map/ppermute | solution.py:45
  315.5 13.4 %collective-permute-start.16 = (f32[2,512,128]{1,2,0:T(8,128)S(1)}, f32[2,512,128]{1,2,0:T(8,128)S(1)}, u32[]{:S(2)}, u32[]{:S(2)}) collective-permute-start(f32[2,512,128]{1,2,0:T(8,128)S(1)} %collective-permute-done.15), channel_id=1, source_target_pairs={{0,4},{4,8},{8,12},{12,16},{16,20},{20,24},{24,28},{28,0},{1,5},{5... | collective-permute-start | bytes 1572872 | tf_op jit(solution)/shard_map/ppermute | solution.py:45
  328.9 12.5 %collective-permute-start.17 = (f32[2,512,128]{1,2,0:T(8,128)S(1)}, f32[2,512,128]{1,2,0:T(8,128)S(1)}, u32[]{:S(2)}, u32[]{:S(2)}) collective-permute-start(f32[2,512,128]{1,2,0:T(8,128)S(1)} %collective-permute-done.16), channel_id=1, source_target_pairs={{0,4},{4,8},{8,12},{12,16},{16,20},{20,24},{24,28},{28,0},{1,5},{5... | collective-permute-start | bytes 1572872 | tf_op jit(solution)/shard_map/ppermute | solution.py:45
  341.3 11.9 %collective-permute-start.18 = (f32[2,512,128]{1,2,0:T(8,128)S(1)}, f32[2,512,128]{1,2,0:T(8,128)S(1)}, u32[]{:S(2)}, u32[]{:S(2)}) collective-permute-start(f32[2,512,128]{1,2,0:T(8,128)S(1)} %collective-permute-done.17), channel_id=1, source_target_pairs={{0,4},{4,8},{8,12},{12,16},{16,20},{20,24},{24,28},{28,0},{1,5},{5... | collective-permute-start | bytes 1572872 | tf_op jit(solution)/shard_map/ppermute | solution.py:45
  354.0 13.1 %collective-permute-start.19 = (f32[2,512,128]{1,2,0:T(8,128)S(1)}, f32[2,512,128]{1,2,0:T(8,128)}, u32[]{:S(2)}, u32[]{:S(2)}) collective-permute-start(f32[2,512,128]{1,2,0:T(8,128)S(1)} %collective-permute-done.18), channel_id=1, source_target_pairs={{0,4},{4,8},{8,12},{12,16},{16,20},{20,24},{24,28},{28,0},{1,5},{5... | collective-permute-start | bytes 1572872 | tf_op jit(solution)/shard_map/ppermute | solution.py:45
  367.1 12.6 %collective-permute-start.20 = (f32[2,512,128]{1,2,0:T(8,128)}, f32[2,512,128]{1,2,0:T(8,128)}, u32[]{:S(2)}, u32[]{:S(2)}) collective-permute-start(f32[2,512,128]{1,2,0:T(8,128)} %collective-permute-done.19), channel_id=1, source_target_pairs={{0,4},{4,8},{8,12},{12,16},{16,20},{20,24},{24,28},{28,0},{1,5},{5... | collective-permute-start | bytes 1572872 | tf_op jit(solution)/shard_map/ppermute | solution.py:45
  367.6 15.6 %copy-start.5 = (f32[2,512,1024]{2,1,0:T(8,128)S(1)}, f32[2,512,1024]{2,1,0:T(8,128)}, u32[]{:S(2)}) copy-start(f32[2,512,1024]{2,1,0:T(8,128)} %param.20) | copy-start | bytes 12582916
  383.2 79.8 %copy-start.26 = (s32[4,64,16]{1,2,0:T(8,128)S(1)}, s32[4,64,16]{1,2,0:T(8,128)}, u32[]{:S(2)}) copy-start(s32[4,64,16]{1,2,0:T(8,128)} %param.26) | copy-start | bytes 49156
  383.3 79.8 %copy-start.27 = (s32[2,64,32]{1,2,0:T(8,128)S(1)}, s32[2,64,32]{1,2,0:T(8,128)}, u32[]{:S(2)}) copy-start(s32[2,64,32]{1,2,0:T(8,128)} %param.27) | copy-start | bytes 49156
  388.4 172.5 %all-reduce.15.cloned.1.call-start = ((), (), s32[]{:S(2)}) async-start(), calls=%async_computation.4 | async-start | bytes 2097152 | tf_op jit(solution)/shard_map/psum | solution.py:86
  419.9 15.4 %collective-permute-start.21 = (f32[2,512,128]{1,2,0:T(8,128)}, f32[2,512,128]{1,2,0:T(8,128)S(1)}, u32[]{:S(2)}, u32[]{:S(2)}) collective-permute-start(f32[2,512,128]{1,2,0:T(8,128)} %all-reduce.11.cloned.1.call-done), channel_id=1, source_target_pairs={{0,4},{4,8},{8,12},{12,16},{16,20},{20,24},{24,28},{28,0},{1,5},{5... | collective-permute-start | bytes 1572872 | tf_op jit(solution)/shard_map/ppermute | solution.py:45
  435.3 14.3 %collective-permute-start.22 = (f32[2,512,128]{1,2,0:T(8,128)S(1)}, f32[2,512,128]{1,2,0:T(8,128)S(1)}, u32[]{:S(2)}, u32[]{:S(2)}) collective-permute-start(f32[2,512,128]{1,2,0:T(8,128)S(1)} %collective-permute-done.21), channel_id=1, source_target_pairs={{0,4},{4,8},{8,12},{12,16},{16,20},{20,24},{24,28},{28,0},{1,5},{5... | collective-permute-start | bytes 1572872 | tf_op jit(solution)/shard_map/ppermute | solution.py:45
  449.6 13.4 %collective-permute-start.23 = (f32[2,512,128]{1,2,0:T(8,128)S(1)}, f32[2,512,128]{1,2,0:T(8,128)S(1)}, u32[]{:S(2)}, u32[]{:S(2)}) collective-permute-start(f32[2,512,128]{1,2,0:T(8,128)S(1)} %collective-permute-done.22), channel_id=1, source_target_pairs={{0,4},{4,8},{8,12},{12,16},{16,20},{20,24},{24,28},{28,0},{1,5},{5... | collective-permute-start | bytes 1572872 | tf_op jit(solution)/shard_map/ppermute | solution.py:45
  463.0 12.5 %collective-permute-start.24 = (f32[2,512,128]{1,2,0:T(8,128)S(1)}, f32[2,512,128]{1,2,0:T(8,128)S(1)}, u32[]{:S(2)}, u32[]{:S(2)}) collective-permute-start(f32[2,512,128]{1,2,0:T(8,128)S(1)} %collective-permute-done.23), channel_id=1, source_target_pairs={{0,4},{4,8},{8,12},{12,16},{16,20},{20,24},{24,28},{28,0},{1,5},{5... | collective-permute-start | bytes 1572872 | tf_op jit(solution)/shard_map/ppermute | solution.py:45
  475.5 1.5 copy-start.20
  475.5 12.6 %collective-permute-start.25 = (f32[2,512,128]{1,2,0:T(8,128)S(1)}, f32[2,512,128]{1,2,0:T(8,128)S(1)}, u32[]{:S(2)}, u32[]{:S(2)}) collective-permute-start(f32[2,512,128]{1,2,0:T(8,128)S(1)} %collective-permute-done.24), channel_id=1, source_target_pairs={{0,4},{4,8},{8,12},{12,16},{16,20},{20,24},{24,28},{28,0},{1,5},{5... | collective-permute-start | bytes 1572872 | tf_op jit(solution)/shard_map/ppermute | solution.py:45
  488.1 13.4 %collective-permute-start.26 = (f32[2,512,128]{1,2,0:T(8,128)S(1)}, f32[2,512,128]{1,2,0:T(8,128)}, u32[]{:S(2)}, u32[]{:S(2)}) collective-permute-start(f32[2,512,128]{1,2,0:T(8,128)S(1)} %collective-permute-done.25), channel_id=1, source_target_pairs={{0,4},{4,8},{8,12},{12,16},{16,20},{20,24},{24,28},{28,0},{1,5},{5... | collective-permute-start | bytes 1572872 | tf_op jit(solution)/shard_map/ppermute | solution.py:45
  488.1 13.5 %copy-start.3 = (f32[4,2048,128]{1,2,0:T(8,128)S(1)}, f32[4,2048,128]{1,2,0:T(8,128)}, u32[]{:S(2)}) copy-start(f32[4,2048,128]{1,2,0:T(8,128)} %copy-done.2) | copy-start | bytes 12582916
  488.1 29.2 %slice-start.2 = ((s8[8388608]{0:T(1024)(128)(4,1)}), s8[4194304]{0:T(1024)(128)(4,1)S(1)}, s32[]{:S(2)}) async-start(s8[8388608]{0:T(1024)(128)(4,1)} %bitcast.57), calls=%async_computation.7 | async-start | bytes 8388608
  489.4 27.6 %copy-start.21 = (f32[2,512,128]{1,2,0:T(8,128)S(1)}, f32[2,512,128]{1,2,0:T(8,128)}, u32[]{:S(2)}) copy-start(f32[2,512,128]{1,2,0:T(8,128)} %copy-done.20) | copy-start | bytes 1572868
  489.4 27.9 %slice-start.3 = ((s8[8388608]{0:T(1024)(128)(4,1)}), s8[4194304]{0:T(1024)(128)(4,1)S(1)}, s32[]{:S(2)}) async-start(s8[8388608]{0:T(1024)(128)(4,1)} %bitcast.57), calls=%async_computation.8 | async-start | bytes 8388608
  501.5 12.3 %collective-permute-start.27 = (f32[2,512,128]{1,2,0:T(8,128)}, f32[2,512,128]{1,2,0:T(8,128)}, u32[]{:S(2)}, u32[]{:S(2)}) collective-permute-start(f32[2,512,128]{1,2,0:T(8,128)} %collective-permute-done.26), channel_id=1, source_target_pairs={{0,4},{4,8},{8,12},{12,16},{16,20},{20,24},{24,28},{28,0},{1,5},{5... | collective-permute-start | bytes 1572872 | tf_op jit(solution)/shard_map/ppermute | solution.py:45
  511.8 5.4 copy-start.7
  517.3 43.6 %copy-start.24 = (f32[1024,128]{1,0:T(8,128)S(1)}, f32[1024,128]{1,0:T(8,128)}, u32[]{:S(2)}) copy-start(f32[1024,128]{1,0:T(8,128)} %param.18) | copy-start | bytes 1572868
  525.0 182.6 %all-reduce.13.cloned.1.call-start = ((), (), s32[]{:S(2)}) async-start(), calls=%async_computation.3 | async-start | bytes 1048576 | tf_op jit(solution)/shard_map/psum | solution.py:56
  562.2 16.2 %collective-permute-start.28 = (f32[1,1024,128]{2,1,0:T(8,128)S(1)}, f32[1,1024,128]{2,1,0:T(8,128)S(1)}, u32[]{:S(2)}, u32[]{:S(2)}) collective-permute-start(f32[1,1024,128]{2,1,0:T(8,128)S(1)} %fusion.21), channel_id=1, source_target_pairs={{0,4},{4,8},{8,12},{12,16},{16,20},{20,24},{24,28},{28,0},{1,5},{5... | collective-permute-start | bytes 1572872 | tf_op jit(solution)/shard_map/ppermute | solution.py:45
  578.4 15.3 %collective-permute-start.29 = (f32[1,1024,128]{2,1,0:T(8,128)S(1)}, f32[1,1024,128]{2,1,0:T(8,128)S(1)}, u32[]{:S(2)}, u32[]{:S(2)}) collective-permute-start(f32[1,1024,128]{2,1,0:T(8,128)S(1)} %collective-permute-done.28), channel_id=1, source_target_pairs={{0,4},{4,8},{8,12},{12,16},{16,20},{20,24},{24,28},{28,0},{1,5},{5... | collective-permute-start | bytes 1572872 | tf_op jit(solution)/shard_map/ppermute | solution.py:45
  593.7 14.4 %collective-permute-start.30 = (f32[1,1024,128]{2,1,0:T(8,128)S(1)}, f32[1,1024,128]{2,1,0:T(8,128)S(1)}, u32[]{:S(2)}, u32[]{:S(2)}) collective-permute-start(f32[1,1024,128]{2,1,0:T(8,128)S(1)} %collective-permute-done.29), channel_id=1, source_target_pairs={{0,4},{4,8},{8,12},{12,16},{16,20},{20,24},{24,28},{28,0},{1,5},{5... | collective-permute-start | bytes 1572872 | tf_op jit(solution)/shard_map/ppermute | solution.py:45
  608.1 13.4 %collective-permute-start.31 = (f32[1,1024,128]{2,1,0:T(8,128)S(1)}, f32[1,1024,128]{2,1,0:T(8,128)S(1)}, u32[]{:S(2)}, u32[]{:S(2)}) collective-permute-start(f32[1,1024,128]{2,1,0:T(8,128)S(1)} %collective-permute-done.30), channel_id=1, source_target_pairs={{0,4},{4,8},{8,12},{12,16},{16,20},{20,24},{24,28},{28,0},{1,5},{5... | collective-permute-start | bytes 1572872 | tf_op jit(solution)/shard_map/ppermute | solution.py:45
  622.3 12.5 %collective-permute-start.32 = (f32[1,1024,128]{2,1,0:T(8,128)S(1)}, f32[1,1024,128]{2,1,0:T(8,128)S(1)}, u32[]{:S(2)}, u32[]{:S(2)}) collective-permute-start(f32[1,1024,128]{2,1,0:T(8,128)S(1)} %collective-permute-done.31), channel_id=1, source_target_pairs={{0,4},{4,8},{8,12},{12,16},{16,20},{20,24},{24,28},{28,0},{1,5},{5... | collective-permute-start | bytes 1572872 | tf_op jit(solution)/shard_map/ppermute | solution.py:45
  635.6 12.6 %collective-permute-start.33 = (f32[1,1024,128]{2,1,0:T(8,128)S(1)}, f32[1,1024,128]{2,1,0:T(8,128)}, u32[]{:S(2)}, u32[]{:S(2)}) collective-permute-start(f32[1,1024,128]{2,1,0:T(8,128)S(1)} %collective-permute-done.32), channel_id=1, source_target_pairs={{0,4},{4,8},{8,12},{12,16},{16,20},{20,24},{24,28},{28,0},{1,5},{5... | collective-permute-start | bytes 1572872 | tf_op jit(solution)/shard_map/ppermute | solution.py:45
  648.3 12.2 %collective-permute-start.34 = (f32[1,1024,128]{2,1,0:T(8,128)}, f32[1,1024,128]{2,1,0:T(8,128)}, u32[]{:S(2)}, u32[]{:S(2)}) collective-permute-start(f32[1,1024,128]{2,1,0:T(8,128)} %collective-permute-done.33), channel_id=1, source_target_pairs={{0,4},{4,8},{8,12},{12,16},{16,20},{20,24},{24,28},{28,0},{1,5},{5... | collective-permute-start | bytes 1572872 | tf_op jit(solution)/shard_map/ppermute | solution.py:45
  661.5 6.7 slice-start
  662.8 5.1 copy-start.11
  664.1 3.9 copy-start.9
  665.4 2.8 slice-start.1
  668.2 41.4 %copy-start.1 = (f32[4,256,512]{2,1,0:T(8,128)S(1)}, f32[4,256,512]{2,1,0:T(8,128)}, u32[]{:S(2)}) copy-start(f32[4,256,512]{2,1,0:T(8,128)} %param.19) | copy-start | bytes 6291460
  (8 other events, 6.9 us)
Sparse Core Ops, SparseCore 0:
  120.0 30.2 all-reduce.6
  254.1 30.5 all-reduce.8
  388.5 31.2 all-reduce.10
  525.1 35.7 all-reduce.14
  678.0 29.5 all-reduce.12
